TPU v7x, 256 devices: a whole 4x4x8 slice. The times are simulated.
256 devices in a mesh: samp: 8 (over x, z_hi), feat: 32 (over y, z_lo, core).
Axes of the slice: x: 4, y: 4, z: 8 (z_hi: 2, z_lo: 4; z = z_hi * 4 + z_lo), core: 2. Of those that a mesh axis runs over, the one named last changes fastest.
Arguments:
- embeddings: bfloat16 [8192, 1024], P('samp'), may hold values from -6 to 6
- frequencies: bfloat16 [1024, 8192], P(None, 'feat'), may hold values from -0.1875 to 0.1875
- phases: float32 [8192], P('feat'), may hold values from -3.140625 to 3.140625
- treat_freq: float32 [8192], P('feat'), may hold values from -3.140625 to 3.140625
- treatment: int32 [8192], P('samp'), may hold values from 0 to 1
- flips: int32 [8192], P('samp'), may hold values from 0 to 1
- panel: int32 [1], replicated, may hold values from 0 to 15
Outputs:
- schur: float32 [8192, 8192], P('samp', 'feat')
- panel_factor: float32 [8192, 512], P('samp')
- moment_scaled: float32 [8192], P('feat')
All inputs are finite; a program needn't handle non-finite values.
Results may differ from a plain program's by a relative error of at most 0.0032.
Values may be sent and summed in bfloat16 or wider, within the bound.
No kernel may reach another device: no remote copies, remote signals or barrier semaphores. Data moves between devices by JAX's collectives and lax.ppermute only.
A program may use at most 128 MiB of HBM per device.

v0:
```python
import jax
import jax.numpy as jnp
from jax import lax
from jax.sharding import PartitionSpec as P

PANEL = 512
ridge = 0.1
root_two = 1.4142135623730951


def broadcast(shard, axis, root):
    mine = lax.axis_index(axis) == root
    return lax.psum(jnp.where(mine, shard, jnp.zeros_like(shard)), axis)


def cosine_map(project, phases, treat_freq, treated):
    return root_two * jnp.cos(project + phases[None, :] + treated[:, None] * treat_freq[None, :])


def inner_rows(left, right):
    return lax.dot_general(
        left, right, (((0,), (0,)), ((), ())), preferred_element_type=jnp.float32
    )


def per_device(embeddings, frequencies, phases, treat_freq, treatment, flips, panel):
    project = jnp.dot(embeddings, frequencies, preferred_element_type=jnp.float32)
    treated = treatment.astype(jnp.float32)
    flipped = flips.astype(jnp.float32)
    counter = treated + flipped - 2.0 * treated * flipped
    observed = cosine_map(project, phases, treat_freq, treated)
    counterfactual = cosine_map(project, phases, treat_freq, counter)
    feature_obs = observed.astype(jnp.bfloat16)
    samp_size = lax.axis_size("samp")
    feat_size = lax.axis_size("feat")
    sample_count = embeddings.shape[0] * samp_size
    col_width = feature_obs.shape[1]
    feat_total = col_width * feat_size
    row_height = feat_total // samp_size
    samp_index = lax.axis_index("samp")
    feat_index = lax.axis_index("feat")
    moment_part = jnp.sum(counterfactual - observed, axis=0)
    moment_sum = lax.psum(moment_part, "samp") / sample_count
    first_col = panel[0] * PANEL
    panel_devs = PANEL // col_width
    first_dev = first_col // col_width
    gram_part = inner_rows(lax.all_gather(feature_obs, "feat", axis=1, tiled=True), feature_obs)
    gram_raw = lax.psum_scatter(gram_part, "samp", scatter_dimension=0, tiled=True)
    row_ids = samp_index * row_height + lax.broadcasted_iota(jnp.int32, (row_height, col_width), 0)
    col_ids = feat_index * col_width + lax.broadcasted_iota(jnp.int32, (row_height, col_width), 1)
    gram_own = gram_raw / sample_count + ridge * (row_ids == col_ids).astype(jnp.float32)
    col_parts = []
    moment_parts = []
    for member in range(panel_devs):
        got_cols, got_moment = (
            broadcast(gram_own, "feat", first_dev + member),
            broadcast(moment_sum, "feat", first_dev + member),
        )
        col_parts.append(got_cols)
        moment_parts.append(got_moment)
    panel_cols = jnp.concatenate(col_parts, axis=1)
    moment_panel = jnp.concatenate(moment_parts, axis=0)
    source_samp = first_col // row_height
    offset_row = first_col % row_height
    pivot_local = lax.dynamic_slice_in_dim(panel_cols, offset_row, PANEL, 0)
    cross_local = lax.dynamic_slice_in_dim(gram_own, offset_row, PANEL, 0)
    pivot, cross = (
        broadcast(pivot_local, "samp", source_samp),
        broadcast(cross_local, "samp", source_samp),
    )
    lower = jnp.linalg.cholesky(pivot)
    factor_t = lax.linalg.triangular_solve(lower, panel_cols.T, left_side=True, lower=True)
    panel_factor = factor_t.T
    cross_t = lax.linalg.triangular_solve(lower, cross, left_side=True, lower=True)
    schur = gram_own - jnp.dot(panel_factor, cross_t, precision=lax.Precision.HIGHEST)
    solved = lax.linalg.triangular_solve(lower, moment_panel[:, None], left_side=True, lower=True)[
        :, 0
    ]
    reduced = moment_sum - jnp.dot(cross_t.T, solved, precision=lax.Precision.HIGHEST)
    moment_scaled = jnp.sqrt(jnp.float32(sample_count)) * reduced
    return (schur, panel_factor, moment_scaled)


def solution(mesh):
    return jax.shard_map(
        per_device,
        mesh=mesh,
        in_specs=(
            P("samp", None),
            P(None, "feat"),
            P("feat"),
            P("feat"),
            P("samp"),
            P("samp"),
            P(),
        ),
        out_specs=(P("samp", "feat"), P("samp", None), P("feat")),
        check_vma=False,
    )
```

profile of v0, /device:TPU:8, one launch (start us, length us, event | category | flops | bytes accessed | tf_op | source)
XLA Modules:
  0.0 977.7 jit_solution(12588586258870872119)
XLA Ops:
  7.2 0.8 convert_element_type.10
  8.1 0.7 multiply_subtract_fusion
  8.8 9.7 subtract_reduce_fusion
  18.5 127.0 %all-gather.2.cloned.1.call-done = bf16[1024,8192]{1,0:T(8,128)(2,1)} async-done(((bf16[1024,256]{1,0:T(8,128)(2,1)}), bf16[1024,8192]{1,0:T(8,128)(2,1)}) %all-gather.2.cloned.1.call-update) | async-done | bytes 16777232 | tf_op jit(solution)/shard_map/all_gather | solution.py:47
  145.5 13.7 %fusion.87 = f32[8192,256]{0,1:T(8,128)} fusion(bf16[1024,8192]{1,0:T(8,128)(2,1)} %all-gather.2.cloned.1.call-done, bf16[1024,256]{1,0:T(8,128)(2,1)} %get-tuple-element.37), kind=kOutput, calls=%fused_computation.148 | convolution fusion | flops 4294967296 | bytes 25690112 | tf_op jit(solution)/shard_map/dot_general | solution.py:21
  160.0 184.1 %reduce-scatter.2.cloned.1.call-done = f32[1024,256]{0,1:T(8,128)} async-done(((f32[8192,256]{0,1:T(8,128)}), f32[1024,256]{0,1:T(8,128)}) %reduce-scatter.2.cloned.1.call-update) | async-done | bytes 1048592 | tf_op jit(solution)/shard_map/reduce_scatter | solution.py:48
  344.1 2.4 broadcast_select_fusion
  346.6 1.1 broadcast_select_fusion.1
  347.9 1.0 dynamic-slice_select_fusion.1
  348.9 263.1 %all-reduce.7.cloned.1.call-done = (f32[1024,256]{0,1:T(8,128)}, f32[1024,256]{0,1:T(8,128)}) async-done(((f32[1024,256]{0,1:T(8,128)}, f32[1024,256]{0,1:T(8,128)}), (f32[1024,256]{0,1:T(8,128)}, f32[1024,256]{0,1:T(8,128)})) %all-reduce.7.cloned.1.call-update) | async-done | bytes 2097168 | tf_op jit(solution)/shard_map/psum | solution.py:13
  612.0 1.4 constant_dynamic-update-slice_fusion.1
  613.6 1.3 copy-done.1
  614.9 1.3 dynamic-slice_select_fusion
  616.3 29.4 %psum.53 = f32[256]{0:T(256)S(1)} all-reduce(f32[256]{0:T(256)S(1)} %get-tuple-element.36), channel_id=1, replica_groups=mesh['samp'=8,'feat'=32] {'samp'}, use_global_device_ids=true, to_apply=%region_14.15 | all-reduce | flops 256 | bytes 2048 | tf_op jit(solution)/shard_map/psum | solution.py:43
  645.7 73.2 %all-reduce.1 = (f32[256]{0:T(256)S(1)}, f32[256]{0:T(256)S(1)}) all-reduce(f32[256]{0:T(256)S(1)} %get-tuple-element.45, f32[256]{0:T(256)S(1)} %get-tuple-element.44), channel_id=1, replica_groups=mesh['samp'=8,'feat'=32] {'feat'}, use_global_device_ids=true, to_apply=%region_15.16 | all-reduce | flops 512 | bytes 4096 | tf_op jit(solution)/shard_map/psum | solution.py:13
  719.4 72.7 %all-reduce.9.cloned.1.call-done = (f32[512,512]{0,1:T(8,128)}, f32[512,256]{0,1:T(8,128)}) async-done(((f32[512,512]{0,1:T(8,128)}, f32[512,256]{0,1:T(8,128)}), (f32[512,512]{0,1:T(8,128)}, f32[512,256]{0,1:T(8,128)})) %all-reduce.9.cloned.1.call-update) | async-done | bytes 1572880 | tf_op jit(solution)/shard_map/psum | solution.py:13
  792.2 2.6 copy.11
  794.8 1.4 fusion.19
  796.3 1.0 copy-done.7
  797.2 11.7 %cholesky.103 = f32[128,128]{1,0:T(8,128)S(1)} custom-call(f32[128,128]{1,0:T(8,128)S(1)} %cholesky.263), custom_call_target="Cholesky" | custom-call | tf_op jit(solution)/shard_map/jit(cholesky)/cholesky | solution.py:71
  809.0 9.8 %custom-call.34 = f32[1,128,128]{1,2,0:T(8,128)S(1)} custom-call(f32[1,128,128]{2,1,0:T(8,128)S(1)} %get-tuple-element.43), custom_call_target="InvertDiagBlocksLowerTriangular" | custom-call | tf_op jit(solution)/shard_map/jit(cholesky)/cholesky | solution.py:71
  818.8 1.2 fusion.35
  820.0 1.3 convolution_subtract_fusion.3
  821.3 11.7 %cholesky.215 = f32[128,128]{1,0:T(8,128)S(1)} custom-call(f32[128,128]{1,0:T(8,128)S(1)} %cholesky.267), custom_call_target="Cholesky" | custom-call | tf_op jit(solution)/shard_map/jit(cholesky)/cholesky | solution.py:71
  833.6 0.7 copy.14
  834.4 0.7 copy.12
  835.2 10.6 %custom-call.35 = f32[1,128,128]{1,2,0:T(8,128)} custom-call(f32[1,128,128]{2,1,0:T(8,128)S(1)} %get-tuple-element.41), custom_call_target="InvertDiagBlocksLowerTriangular" | custom-call | tf_op jit(solution)/shard_map/jit(cholesky)/cholesky | solution.py:71
  845.7 1.0 cholesky.222
  846.7 0.8 constant_dynamic-update-slice_fusion.3
  847.6 1.2 convolution_dynamic-update-slice_fusion
  848.7 1.5 convolution_subtract_fusion.6
  850.3 11.7 %cholesky.236 = f32[128,128]{1,0:T(8,128)S(1)} custom-call(f32[128,128]{1,0:T(8,128)S(1)} %cholesky.272), custom_call_target="Cholesky" | custom-call | tf_op jit(solution)/shard_map/jit(cholesky)/cholesky | solution.py:71
  862.1 9.8 %custom-call.36 = f32[1,128,128]{1,2,0:T(8,128)S(1)} custom-call(f32[1,128,128]{2,1,0:T(8,128)S(1)} %get-tuple-element.39), custom_call_target="InvertDiagBlocksLowerTriangular" | custom-call | tf_op jit(solution)/shard_map/jit(cholesky)/cholesky | solution.py:71
  872.2 1.3 convolution_subtract_fusion.8
  873.6 11.9 %cholesky.253 = f32[128,128]{1,0:T(8,128)S(1)} custom-call(f32[128,128]{1,0:T(8,128)S(1)} %convolution_subtract_fusion.8), custom_call_target="Cholesky" | custom-call | tf_op jit(solution)/shard_map/jit(cholesky)/cholesky | solution.py:71
  886.2 0.7 compare_reduce_fusion
  886.9 1.3 compare_reduce_fusion.2
  890.7 1.1 select_select_fusion
  891.8 14.1 %while.1 = (s32[]{:T(128)}, f32[512,512]{0,1:T(8,128)}, s32[4,2]{0,1:T(2,128)S(1)}, f32[4,128,128]{2,1,0:T(8,128)}, s32[]{:T(128)}) while((s32[]{:T(128)}, f32[512,512]{0,1:T(8,128)}, s32[4,2]{0,1:T(2,128)S(1)}, f32[4,128,128]{2,1,0:T(8,128)}, s32[]{:T(128)}) %tuple.32), condition=%wide.while_cond, body=%wide.while_body.sunk | while | flops 2 | bytes 393829 | solution.py:72
  892.4 2.2 dynamic-slice.7
  895.9 2.2 dynamic-slice.7
  898.3 0.6 bitcast_dynamic-update-slice_fusion.2
  899.5 2.2 dynamic-slice.7
  903.0 2.2 dynamic-slice.7
  905.3 0.6 bitcast_dynamic-update-slice_fusion.2
  905.9 40.2 %custom-call.37 = f32[4,128,128]{1,2,0:T(8,128)S(1)} custom-call(f32[4,128,128]{2,1,0:T(8,128)} %get-tuple-element.10), custom_call_target="InvertDiagBlocksLowerTriangular" | custom-call | tf_op jit(solution)/shard_map/triangular_solve | solution.py:72
  946.3 1.1 fusion.12
  947.6 1.1 fusion.13
  948.9 1.2 fusion.15
  950.2 1.2 fusion.40
  951.4 1.3 convolution_subtract_fusion.7
  953.1 1.6 convolution_subtract_fusion.5
  955.0 1.7 convolution_subtract_fusion.4
  957.1 0.6 fusion.21
  957.7 0.6 convolution_subtract_fusion.2
  958.4 0.6 fusion.53
  959.0 0.7 convolution_subtract_fusion.1
  959.7 0.6 fusion.55
  960.4 1.1 fusion.6
  961.5 0.6 fusion.57
  962.2 1.6 fusion.9
  963.8 2.0 convolution_subtract_fusion
  966.8 2.9 copy.22
  969.6 1.3 copy.21
  (71 shorter events, 9.6 us)
Async XLA Ops:
  7.2 1.6 copy-start
  7.2 138.3 %all-gather.2.cloned.1.call-start = ((), (), s32[]{:S(2)}) async-start(), calls=%async_computation.1 | async-start | bytes 17301504 | tf_op jit(solution)/shard_map/all_gather | solution.py:47
  18.5 325.7 %reduce-scatter.2.cloned.1.call-start = ((), (), s32[]{:S(2)}) async-start(), calls=%async_computation.2 | async-start | bytes 9437184 | tf_op jit(solution)/shard_map/reduce_scatter | solution.py:48
  159.2 452.7 %all-reduce.7.cloned.1.call-start = ((), (), s32[]{:S(2)}) async-start(), calls=%async_computation.3 | async-start | bytes 4194304 | tf_op jit(solution)/shard_map/psum | solution.py:13
  346.6 1.3 copy-start.3
  347.7 444.5 %all-reduce.9.cloned.1.call-start = ((), (), s32[]{:S(2)}) async-start(), calls=%async_computation.4 | async-start | bytes 3145728 | tf_op jit(solution)/shard_map/psum | solution.py:13
  612.0 1.5 copy-start.8
  613.6 1.3 copy-start.1
  792.2 2.6 copy-start.6
  796.3 1.0 copy-start.7
  848.7 43.0 %copy-start.9 = (s32[4]{0:T(128)S(1)}, s32[4]{0:T(128)}, u32[]{:S(2)}) copy-start(s32[4]{0:T(128)} %iota_multiply_fusion) | copy-start | bytes 52
  905.9 49.1 %copy-start.5 = (f32[512,512]{0,1:T(8,128)S(1)}, f32[512,512]{0,1:T(8,128)}, u32[]{:S(2)}) copy-start(f32[512,512]{0,1:T(8,128)} %get-tuple-element.104) | copy-start | bytes 3145732
  946.1 10.9 %copy-start.2 = (f32[1024,512]{0,1:T(8,128)S(1)}, f32[1024,512]{0,1:T(8,128)}, u32[]{:S(2)}) copy-start(f32[1024,512]{0,1:T(8,128)} %copy-done.1) | copy-start | bytes 6291460
  962.1 1.6 copy-start.4
Sparse Core Ops, SparseCore 0:
  18.6 126.8 all-gather.1
  159.4 184.7 reduce-scatter.1
  347.8 264.0 all-reduce.6
  616.4 175.7 all-reduce.8
where the time goes:
time: 985 us; the launch traced here: 978 us
  waiting for transfers between devices  647 us (66%)
  other arithmetic  133 us (14%)
  blocking collectives  103 us (10%)
  matrix products  48.4 us (5%)
  local copies, waits for them, and re-layouts  28.5 us (3%)
  between operations  17.5 us (2%)
    psum x2, waiting for transfers between devices, broadcast(): return lax.psum(jnp.where(mine, shard, jnp.zeros_like(shard)), axis)  336 us
    reduce_scatter x1, waiting for transfers between devices, per_device(): lax.psum_scatter(gram_part, 'samp', scatter_dimension=0, tiled=True)  184 us
    all_gather x1, waiting for transfers between devices, per_device(): lax.all_gather(feature_obs, 'feat', axis=1, tiled=True)  127 us
    another operation x14, other arithmetic, per_device(): lower = jnp.linalg.cholesky(pivot)  80.5 us
    psum x1, blocking collectives, broadcast(): return lax.psum(jnp.where(mine, shard, jnp.zeros_like(shard)), axis)  73.2 us
    another operation x3, other arithmetic, per_device(): lax.linalg.triangular_solve(lower, panel_cols.T, left_side=True, lower=True)  41.9 us
    psum x1, blocking collectives, per_device(): moment_sum = lax.psum(moment_part, 'samp') / sample_count  29.4 us
  transfers between devices with their start and end apart: 4, of which 4 were waited for; matrix products, arithmetic and copies ran while one was open for 0% of the time, Pallas kernels for 0%

commit v1 on v0

--- a/solution.py
+++ b/solution.py
@@ -44,7 +44,12 @@
     first_col = panel[0] * PANEL
     panel_devs = PANEL // col_width
     first_dev = first_col // col_width
-    gram_part = inner_rows(lax.all_gather(feature_obs, "feat", axis=1, tiled=True), feature_obs)
+    gram_part = inner_rows(
+        jnp.concatenate(
+            lax.all_to_all(jnp.stack([feature_obs] * lax.axis_size("feat")), "feat", 0, 0), axis=1
+        ),
+        feature_obs,
+    )
     gram_raw = lax.psum_scatter(gram_part, "samp", scatter_dimension=0, tiled=True)
     row_ids = samp_index * row_height + lax.broadcasted_iota(jnp.int32, (row_height, col_width), 0)
     col_ids = feat_index * col_width + lax.broadcasted_iota(jnp.int32, (row_height, col_width), 1)

time: 985 us -> 1220 us (1.24)
  blocking collectives: 103 us -> 474 us
  waiting for transfers between devices: 647 us -> 524 us
    all_to_all x0 -> x1, blocking collectives: none -> 372 us  [per_device(): lax.all_to_all(jnp.stack([feature_obs] * lax.axis_size('feat')), 'feat',...]
    all_gather x1 -> x0, waiting for transfers between devices: 127 us -> none  [per_device(): lax.all_gather(feature_obs, 'feat', axis=1, tiled=True)]
  transfers between devices with their start and end apart: 4 -> 3, of which waited for: 4 -> 3; matrix products, arithmetic and copies ran while one was open for 0% -> 0% of each run, Pallas kernels for 0% -> 0%
where the time goes in v1:
time: 1220 us; the launch traced here: 1210 us
  waiting for transfers between devices  524 us (43%)
  blocking collectives  474 us (39%)
  other arithmetic  131 us (11%)
  matrix products  41.9 us (3%)
  local copies, waits for them, and re-layouts  23.3 us (2%)
  between operations  17.6 us (1%)
    all_to_all x1, blocking collectives, per_device(): lax.all_to_all(jnp.stack([feature_obs] * lax.axis_size('feat')), 'feat',...  372 us
    psum x2, waiting for transfers between devices, broadcast(): return lax.psum(jnp.where(mine, shard, jnp.zeros_like(shard)), axis)  337 us
    reduce_scatter x1, waiting for transfers between devices, per_device(): lax.psum_scatter(gram_part, 'samp', scatter_dimension=0, tiled=True)  187 us
    another operation x14, other arithmetic, per_device(): lower = jnp.linalg.cholesky(pivot)  78.9 us
    psum x1, blocking collectives, broadcast(): return lax.psum(jnp.where(mine, shard, jnp.zeros_like(shard)), axis)  73.2 us
    another operation x3, other arithmetic, per_device(): lax.linalg.triangular_solve(lower, panel_cols.T, left_side=True, lower=True)  40.3 us
    psum x1, blocking collectives, per_device(): moment_sum = lax.psum(moment_part, 'samp') / sample_count  29.4 us
  transfers between devices with their start and end apart: 3, of which 3 were waited for; matrix products, arithmetic and copies ran while one was open for 0% of the time, Pallas kernels for 0%

profile of v1, /device:TPU:8, one launch (start us, length us, event | category | flops | bytes accessed | tf_op | source)
XLA Modules:
  0.0 1211.7 jit_solution(16973379749833338783)
XLA Ops:
  7.2 0.8 convert_element_type.10
  8.1 0.7 multiply_subtract_fusion
  8.8 8.6 subtract_reduce_fusion
  17.6 2.2 stack.2
  19.8 371.6 %all_to_all.5 = bf16[32,1024,256]{1,2,0:T(8,128)(2,1)} all-to-all(bf16[32,1024,256]{1,2,0:T(8,128)(2,1)S(1)} %stack.2), channel_id=1, replica_groups=mesh['samp'=8,'feat'=32] {'feat'}, dimensions={0} | all-to-all | bytes 33554432 | tf_op jit(solution)/shard_map/all_to_all | solution.py:49
  391.4 13.6 %fusion.87 = f32[8192,256]{0,1:T(8,128)} fusion(bf16[1024,8192]{0,1:T(8,128)(2,1)} %bitcast.119, bf16[1024,256]{1,0:T(8,128)(2,1)S(1)} %get-tuple-element.44), kind=kOutput, calls=%fused_computation.148 | convolution fusion | flops 4294967296 | bytes 25690112 | tf_op jit(solution)/shard_map/dot_general | solution.py:21
  405.7 187.2 %reduce-scatter.2.cloned.1.call-done = f32[1024,256]{0,1:T(8,128)} async-done(((f32[8192,256]{0,1:T(8,128)}), f32[1024,256]{0,1:T(8,128)}) %reduce-scatter.2.cloned.1.call-update) | async-done | bytes 1048592 | tf_op jit(solution)/shard_map/reduce_scatter | solution.py:53
  592.9 2.4 broadcast_select_fusion
  595.3 1.0 broadcast_select_fusion.1
  596.5 1.0 dynamic-slice_select_fusion.1
  597.5 263.2 %all-reduce.7.cloned.1.call-done = (f32[1024,256]{0,1:T(8,128)}, f32[1024,256]{0,1:T(8,128)}) async-done(((f32[1024,256]{0,1:T(8,128)}, f32[1024,256]{0,1:T(8,128)}), (f32[1024,256]{0,1:T(8,128)}, f32[1024,256]{0,1:T(8,128)})) %all-reduce.7.cloned.1.call-update) | async-done | bytes 2097168 | tf_op jit(solution)/shard_map/psum | solution.py:13
  860.7 1.4 constant_dynamic-update-slice_fusion.1
  862.4 1.6 dynamic-slice_select_fusion
  864.0 29.4 %psum.53 = f32[256]{0:T(256)S(1)} all-reduce(f32[256]{0:T(256)S(1)} %get-tuple-element.43), channel_id=1, replica_groups=mesh['samp'=8,'feat'=32] {'samp'}, use_global_device_ids=true, to_apply=%region_14.15 | all-reduce | flops 256 | bytes 2048 | tf_op jit(solution)/shard_map/psum | solution.py:43
  893.3 73.2 %all-reduce.1 = (f32[256]{0:T(256)S(1)}, f32[256]{0:T(256)S(1)}) all-reduce(f32[256]{0:T(256)S(1)} %get-tuple-element.52, f32[256]{0:T(256)S(1)} %get-tuple-element.51), channel_id=1, replica_groups=mesh['samp'=8,'feat'=32] {'feat'}, use_global_device_ids=true, to_apply=%region_15.16 | all-reduce | flops 512 | bytes 4096 | tf_op jit(solution)/shard_map/psum | solution.py:13
  966.6 73.4 %all-reduce.9.cloned.1.call-done = (f32[512,512]{0,1:T(8,128)}, f32[512,256]{0,1:T(8,128)}) async-done(((f32[512,512]{0,1:T(8,128)}, f32[512,256]{0,1:T(8,128)}), (f32[512,512]{0,1:T(8,128)}, f32[512,256]{0,1:T(8,128)})) %all-reduce.9.cloned.1.call-update) | async-done | bytes 1572880 | tf_op jit(solution)/shard_map/psum | solution.py:13
  1039.9 2.5 copy.25
  1042.4 1.8 fusion.19
  1044.2 1.0 copy-done.4
  1045.2 11.7 cholesky.103
  1056.9 9.8 custom-call.34
  1066.8 1.2 fusion.35
  1068.0 1.3 convolution_subtract_fusion.3
  1069.3 11.7 cholesky.215
  1081.4 10.2 custom-call.35
  1092.0 1.5 convolution_subtract_fusion.6
  1093.6 11.7 cholesky.236
  1105.4 9.8 custom-call.36
  1115.5 1.3 convolution_subtract_fusion.8
  1116.9 11.9 cholesky.253
  1128.9 0.6 compare_reduce_fusion.1
  1129.5 0.7 compare_reduce_fusion
  1130.2 0.6 compare_reduce_fusion.2
  1133.6 10.8 while.1
  1133.7 0.5 fusion.106
  1134.2 1.4 dynamic-slice.7
  1135.7 0.6 bitcast_dynamic-update-slice_fusion.2
  1136.4 0.5 fusion.106
  1136.9 1.4 dynamic-slice.7
  1138.4 0.6 bitcast_dynamic-update-slice_fusion.2
  1139.1 0.5 fusion.106
  1139.6 1.4 dynamic-slice.7
  1141.1 0.6 bitcast_dynamic-update-slice_fusion.2
  1141.8 0.5 fusion.106
  1142.3 1.4 dynamic-slice.7
  1143.8 0.6 bitcast_dynamic-update-slice_fusion.2
  1144.4 40.1 %custom-call.37 = f32[4,128,128]{1,2,0:T(8,128)S(1)} custom-call(f32[4,128,128]{2,1,0:T(8,128)} %get-tuple-element.10), custom_call_target="InvertDiagBlocksLowerTriangular" | custom-call | tf_op jit(solution)/shard_map/triangular_solve | solution.py:77
  1185.8 0.3 fusion.40
  1186.2 0.4 convolution_subtract_fusion.7
  1186.9 0.6 convolution_subtract_fusion.5
  1187.8 0.8 convolution_subtract_fusion.4
  1189.0 1.7 fusion.21
  1190.7 0.6 convolution_subtract_fusion.2
  1191.3 0.6 fusion.53
  1191.9 0.7 convolution_subtract_fusion.1
  1192.7 0.6 fusion.55
  1193.3 1.1 fusion.6
  1194.4 0.6 fusion.57
  1195.1 1.6 fusion.9
  1196.7 3.0 convolution_subtract_fusion
  1199.7 0.3 fusion.23
  1200.0 0.6 subtract_multiply_fusion
  1200.6 3.0 copy.36
  1203.7 1.3 copy.35
  (67 shorter events, 5.1 us)
Async XLA Ops:
  7.2 1.6 copy-start
  7.2 585.7 %reduce-scatter.2.cloned.1.call-start = ((), (), s32[]{:S(2)}) async-start(), calls=%async_computation.2 | async-start | bytes 9437184 | tf_op jit(solution)/shard_map/reduce_scatter | solution.py:53
  405.0 455.7 %all-reduce.7.cloned.1.call-start = ((), (), s32[]{:S(2)}) async-start(), calls=%async_computation.3 | async-start | bytes 4194304 | tf_op jit(solution)/shard_map/psum | solution.py:13
  596.4 443.5 %all-reduce.9.cloned.1.call-start = ((), (), s32[]{:S(2)}) async-start(), calls=%async_computation.4 | async-start | bytes 3145728 | tf_op jit(solution)/shard_map/psum | solution.py:13
  860.7 1.5 copy-start.5
  862.4 180.1 %copy-start.2 = (f32[1024,512]{0,1:T(8,128)}, f32[1024,512]{0,1:T(8,128)S(1)}, u32[]{:S(2)}) copy-start(f32[1024,512]{0,1:T(8,128)S(1)} %constant_dynamic-update-slice_fusion) | copy-start | bytes 6291460
  1044.2 1.0 copy-start.4
  1133.6 52.3 %copy-start.7 = (f32[512,256]{0,1:T(8,128)S(1)}, f32[512,256]{0,1:T(8,128)}, u32[]{:S(2)}) copy-start(f32[512,256]{0,1:T(8,128)} %get-tuple-element.38) | copy-start | bytes 1572868
  1186.2 4.5 copy-start.3
  1200.6 3.0 copy-start.6
  1200.6 4.3 copy-start.1
Sparse Core Ops, SparseCore 0:
  405.1 187.7 reduce-scatter.1
  596.5 264.1 all-reduce.6
  864.2 175.6 all-reduce.8
